TPU v7x, 512 devices: a whole 4x4x16 slice. The times are simulated.
512 devices in a mesh: aux: 32 (over z, y_hi), pair: 16 (over x, y_lo, core).
Axes of the slice: x: 4, y: 4 (y_hi: 2, y_lo: 2; y = y_hi * 2 + y_lo), z: 16, core: 2. Of those that a mesh axis runs over, the one named last changes fastest.
Arguments:
- half_ints: bfloat16 [96, 1408, 4096], P('pair', None, 'aux'), may hold values from -0.75 to 0.75
- vir_coeffs: bfloat16 [1408, 1280], P(None, 'aux'), may hold values from -0.15625 to 0.15625
- occ_energy: float32 [96], replicated, may hold values from -2 to -0.3
- vir_energy: float32 [1280], replicated, may hold values from 0.3 to 4
- roster: int32 [32, 2], replicated, may hold values from 0 to 15
Outputs:
- density: bfloat16 [1280, 96, 4096], P('pair', 'aux')
All inputs are finite; a program needn't handle non-finite values.
Results may differ from a plain program's by a relative error of at most 0.0058.
Values may be sent and summed in bfloat16 or wider, within the bound.
A program may use at most 64 MiB of HBM per device.

v0:
```python
import jax
import jax.numpy as jnp
from jax import lax
from jax.sharding import PartitionSpec as P

spin_scale = 1.3


def broadcast(value, axis, source):
    kept = jnp.where(lax.axis_index(axis) == source, value, 0).astype(value.dtype)
    return lax.psum(kept, axis)


def per_device(half_ints, vir_coeffs, occ_energy, vir_energy, roster):
    occ_rows = half_ints.shape[0]
    aux_slice = half_ints.shape[2]
    half_flat = jnp.transpose(half_ints, (1, 0, 2)).reshape(
        half_ints.shape[1], occ_rows * aux_slice
    )
    columns = lax.all_gather(vir_coeffs, "aux", axis=1, tiled=True)
    product = jnp.dot(jnp.transpose(columns), half_flat, preferred_element_type=jnp.float32)
    vir_ints = product.astype(jnp.bfloat16).reshape(columns.shape[1], occ_rows, aux_slice)
    by_virtual = lax.all_to_all(vir_ints, "pair", split_axis=0, concat_axis=1, tiled=True)
    aux_count = lax.axis_size("aux")
    aux_index = lax.axis_index("aux")
    pair_index = lax.axis_index("pair")
    vir_width = by_virtual.shape[0]
    occ_width = by_virtual.shape[1] // aux_count
    step_count = roster.shape[1]
    block_plan = lax.dynamic_index_in_dim(roster, aux_index, 0, keepdims=False)
    sources = []
    for position in range(step_count):
        sources.append(lax.dynamic_index_in_dim(block_plan, position, 0, keepdims=False))
    own_block = lax.all_to_all(by_virtual, "aux", split_axis=1, concat_axis=2, tiled=True)
    remotes = [broadcast(own_block, "pair", source) for source in sources]
    aux_total = own_block.shape[2]
    flat_local = own_block.reshape(vir_width * occ_width, aux_total)
    occ_block = lax.dynamic_slice_in_dim(occ_energy, aux_index * occ_width, occ_width, 0)
    vir_block = lax.dynamic_slice_in_dim(vir_energy, pair_index * vir_width, vir_width, 0)
    energy_left = (vir_block[:, None] - occ_block[None, :]).reshape(-1)
    density = jnp.zeros((vir_width * occ_width, aux_total), jnp.float32)
    for position in range(step_count):
        flat_remote = remotes[position].reshape(vir_width * occ_width, aux_total)
        energy_block = lax.dynamic_slice_in_dim(
            vir_energy, sources[position] * vir_width, vir_width, 0
        )
        energy_right = (energy_block[:, None] - occ_block[None, :]).reshape(-1)
        integrals = jnp.dot(
            flat_local, jnp.transpose(flat_remote), preferred_element_type=jnp.float32
        )
        amplitudes = (
            spin_scale * integrals / (energy_left[:, None] + energy_right[None, :])
        ).astype(jnp.bfloat16)
        density = density + jnp.dot(amplitudes, flat_remote, preferred_element_type=jnp.float32)
    return density.astype(jnp.bfloat16).reshape(vir_width, occ_width, aux_total)


def solution(mesh):
    in_specs = (P("pair", None, "aux"), P(None, "aux"), P(), P(), P())
    out_specs = P("pair", "aux", None)
    return jax.shard_map(
        per_device, mesh=mesh, in_specs=in_specs, out_specs=out_specs, check_vma=False
    )
```

profile of v0, /device:TPU:15, one launch (start us, length us, event | category | flops | bytes accessed | tf_op | source)
XLA Modules:
  0.0 497.1 jit_solution(2042534354434699088)
XLA Ops:
  6.5 0.0 copy-start
  6.5 0.7 all-gather.2.cloned.1.call-update
  7.3 2.9 copy.14
  10.2 153.8 %all-gather.2.cloned.1.call-done = bf16[1408,1280]{0,1:T(8,128)(2,1)} async-done(((bf16[1408,40]{0,1:T(8,128)(2,1)}), bf16[1408,1280]{0,1:T(8,128)(2,1)}) %all-gather.2.cloned.1.call-update) | async-done | bytes 3604496 | tf_op jit(solution)/shard_map/all_gather | solution.py:20
  164.0 6.4 %convolution_convert_fusion = bf16[1280,768]{0,1:T(8,128)(2,1)} fusion(bf16[1408,1280]{0,1:T(8,128)(2,1)} %all-gather.2.cloned.1.call-done, bf16[1408,768]{0,1:T(8,128)(2,1)S(1)} %bitcast.58), kind=kOutput, calls=%fused_computation.2 | convolution fusion | flops 2769223680 | bytes 7733248 | tf_op jit(solution)/shard_map/dot_general | solution.py:21
  170.4 3.9 copy.15
  174.3 45.4 %all_to_all.33 = bf16[1280,6,128]{2,1,0:T(8,128)(2,1)S(1)} all-to-all(bf16[1280,6,128]{2,1,0:T(8,128)(2,1)S(1)} %copy.15), channel_id=1, replica_groups=mesh['aux'=32,'pair'=16] {'pair'}, dimensions={0} | all-to-all | bytes 3932160 | tf_op jit(solution)/shard_map/all_to_all | solution.py:23
  219.7 1.5 copy.17
  221.2 7.8 %all-to-all-start.1 = ((bf16[80,96,128]{2,0,1:T(8,128)(2,1)}), bf16[80,96,128]{2,0,1:T(8,128)(2,1)S(1)}, u32[]{:S(2)}, u32[]{:S(2)}) async-start(bf16[80,96,128]{2,0,1:T(8,128)(2,1)} %bitcast.55), calls=%async_computation.1 | async-start | bytes 3932160 | tf_op jit(solution)/shard_map/all_to_all | solution.py:34
  229.0 0.2 all-reduce.3.cloned.1.call-start
  229.3 0.1 constant_dynamic-slice_fusion
  229.3 0.6 fusion.41
  231.2 89.0 %all-to-all-done.1 = bf16[80,96,128]{2,0,1:T(8,128)(2,1)S(1)} async-done(((bf16[80,96,128]{2,0,1:T(8,128)(2,1)}), bf16[80,96,128]{2,0,1:T(8,128)(2,1)S(1)}, u32[]{:S(2)}, u32[]{:S(2)}) %all-to-all-start.1) | async-done | bytes 1966112 | tf_op jit(solution)/shard_map/all_to_all | solution.py:34
  320.2 0.3 broadcast_select_fusion
  320.4 1.0 copy-done.1
  321.4 0.5 copy.20
  322.0 0.5 copy.19
  322.5 5.2 %copy_bitcast_fusion = (bf16[240,4096]{1,0:T(8,128)(2,1)}, bf16[240,4096]{1,0:T(8,128)(2,1)}) fusion(bf16[30,8,32,128]{3,2,1,0:T(8,128)(2,1)S(1)} %bitcast.56, bf16[30,8,32,128]{3,2,1,0:T(8,128)(2,1)S(1)} %bitcast.57), kind=kLoop, calls=%fused_computation.3 | loop fusion | bytes 7864320 | tf_op jit(solution)/shard_map/reshape | solution.py:43
  327.7 0.0 all-reduce.3.cloned.1.call-update
  329.0 0.0 copy-done.2
  329.0 0.1 dynamic_slice.26
  329.1 0.9 fusion.40
  329.9 0.1 broadcast_subtract_fusion
  330.0 0.2 sub.65
  330.2 0.2 sub.59
  330.4 0.2 sub.62
  330.5 2.1 copy.18
  332.6 137.9 %all-reduce.3.cloned.1.call-done = (bf16[240,4096]{1,0:T(8,128)(2,1)}, bf16[240,4096]{1,0:T(8,128)(2,1)}) async-done(((bf16[240,4096]{1,0:T(8,128)(2,1)}, bf16[240,4096]{1,0:T(8,128)(2,1)}), (bf16[240,4096]{1,0:T(8,128)(2,1)}, bf16[240,4096]{1,0:T(8,128)(2,1)})) %all-reduce.3.cloned.1.call-update) | async-done | bytes 3932176 | tf_op jit(solution)/shard_map/psum | solution.py:11
  470.5 6.4 %fusion.26 = f32[240,4096]{1,0:T(8,128)} fusion(bf16[240,4096]{1,0:T(8,128)(2,1)} %get-tuple-element.5, bf16[30,8,32,128]{3,2,1,0:T(8,128)(2,1)S(1)} %bitcast.50, f32[240]{0:T(256)S(1)} %sub.62, f32[240]{0:T(256)S(1)} %sub.59), kind=kOutput, calls=%fused_computation.19 | convolution fusion | flops 943948800 | bytes 7866240 | tf_op jit(solution)/shard_map/dot_general | solution.py:54
  476.8 7.0 %fusion = bf16[240,4096]{1,0:T(8,128)(2,1)} fusion(f32[240,4096]{1,0:T(8,128)} %fusion.26, bf16[240,4096]{1,0:T(8,128)(2,1)} %get-tuple-element.6, bf16[30,8,32,128]{3,2,1,0:T(8,128)(2,1)S(1)} %bitcast.51, f32[240]{0:T(256)S(1)} %sub.65, f32[240]{0:T(256)S(1)} %sub.59), kind=kOutput, calls=%fused_computation.1 | convolution fusion | flops 945914880 | bytes 9832320 | tf_op jit(solution)/shard_map/dot_general | solution.py:54
  483.8 3.7 reshape.80
  487.5 2.7 copy.21
  (4 shorter events, 0.0 us)
Async XLA Ops:
  6.5 222.7 %copy-start = (s32[32,2]{0,1:T(2,128)S(1)}, s32[32,2]{0,1:T(2,128)}, u32[]{:S(2)}) copy-start(s32[32,2]{0,1:T(2,128)} %param.9) | copy-start | bytes 772
  6.5 157.5 %all-gather.2.cloned.1.call-start = ((), (), s32[]{:S(2)}) async-start(), calls=%async_computation.2 | async-start | bytes 3717120 | tf_op jit(solution)/shard_map/all_gather | solution.py:20
  221.2 99.0 %all-to-all-start.1 = ((bf16[80,96,128]{2,0,1:T(8,128)(2,1)}), bf16[80,96,128]{2,0,1:T(8,128)(2,1)S(1)}, u32[]{:S(2)}, u32[]{:S(2)}) async-start(bf16[80,96,128]{2,0,1:T(8,128)(2,1)} %bitcast.55), calls=%async_computation.1 | async-start | bytes 3932160 | tf_op jit(solution)/shard_map/all_to_all | solution.py:34
  229.0 241.4 %all-reduce.3.cloned.1.call-start = ((), (), s32[]{:S(2)}) async-start(), calls=%async_computation.3 | async-start | bytes 7864320 | tf_op jit(solution)/shard_map/psum | solution.py:11
  320.2 1.3 copy-start.1
  327.7 1.3 copy-start.2
Sparse Core Ops, SparseCore 0:
  10.5 153.4 all-gather.1
  327.9 142.5 all-reduce.2
where the time goes:
time: 498 us; the launch traced here: 497 us
  waiting for transfers between devices  381 us (77%)
  blocking collectives  45.4 us (9%)
  local copies, waits for them, and re-layouts  26.1 us (5%)
  matrix products  19.8 us (4%)
  between operations  16 us (3%)
  starting transfers between devices  8.03 us (2%)
    all_gather x1, waiting for transfers between devices, per_device(): columns = lax.all_gather(vir_coeffs, 'aux', axis=1, tiled=True)  154 us
    psum x1, waiting for transfers between devices, broadcast(): return lax.psum(kept, axis)  138 us
    all_to_all x1, waiting for transfers between devices, per_device(): lax.all_to_all(by_virtual, 'aux', split_axis=1, concat_axis=2, tiled=True)  89 us
    all_to_all x1, blocking collectives, per_device(): lax.all_to_all(vir_ints, 'pair', split_axis=0, concat_axis=1, tiled=True)  45.4 us
    dot_general x2, matrix products, per_device(): jnp.dot(amplitudes, flat_remote, preferred_element_type=jnp.float32)  13.3 us
  transfers between devices with their start and end apart: 3, of which 3 were waited for; matrix products, arithmetic and copies ran while one was open for 1% of the time, Pallas kernels for 0%

commit v1 on v0

--- a/solution.py
+++ b/solution.py
@@ -17,7 +17,15 @@
     half_flat = jnp.transpose(half_ints, (1, 0, 2)).reshape(
         half_ints.shape[1], occ_rows * aux_slice
     )
-    columns = lax.all_gather(vir_coeffs, "aux", axis=1, tiled=True)
+    columns = jnp.concatenate(
+        lax.all_to_all(
+            jnp.stack([vir_coeffs for _ in range(lax.axis_size("aux"))], 0),
+            axis_name="aux",
+            split_axis=0,
+            concat_axis=0,
+        ),
+        1,
+    )
     product = jnp.dot(jnp.transpose(columns), half_flat, preferred_element_type=jnp.float32)
     vir_ints = product.astype(jnp.bfloat16).reshape(columns.shape[1], occ_rows, aux_slice)
     by_virtual = lax.all_to_all(vir_ints, "pair", split_axis=0, concat_axis=1, tiled=True)

time: 498 us -> 513 us (1.030)
  starting transfers between devices: 8.03 us -> 27.8 us
  blocking collectives: 45.4 us -> 35.3 us
    all_to_all x0 -> x1, waiting for transfers between devices: none -> 157 us  [per_device(): lax.all_to_all(jnp.stack([vir_coeffs for _ in range(lax.axis_size('aux'))...]
    all_gather x1 -> x0, waiting for transfers between devices: 154 us -> none  [per_device(): columns = lax.all_gather(vir_coeffs, 'aux', axis=1, tiled=True)]
    all_to_all x0 -> x1, starting transfers between devices: none -> 17.2 us  [per_device(): lax.all_to_all(jnp.stack([vir_coeffs for _ in range(lax.axis_size('aux'))...]
    all_to_all x1, blocking collectives: 45.4 us -> 35.3 us  [per_device(): lax.all_to_all(vir_ints, 'pair', split_axis=0, concat_axis=1, tiled=True)]
where the time goes in v1:
time: 513 us
  waiting for transfers between devices  384 us (75%)
  blocking collectives  35.3 us (7%)
  local copies, waits for them, and re-layouts  28.7 us (6%)
  starting transfers between devices  27.8 us (5%)
  matrix products  20.6 us (4%)
  between operations  16 us (3%)
    all_to_all x1, waiting for transfers between devices, per_device(): lax.all_to_all(jnp.stack([vir_coeffs for _ in range(lax.axis_size('aux'))...  157 us
    psum x1, waiting for transfers between devices, broadcast(): return lax.psum(kept, axis)  138 us
    all_to_all x1, waiting for transfers between devices, per_device(): lax.all_to_all(by_virtual, 'aux', split_axis=1, concat_axis=2, tiled=True)  89 us
    all_to_all x1, blocking collectives, per_device(): lax.all_to_all(vir_ints, 'pair', split_axis=0, concat_axis=1, tiled=True)  35.3 us
    all_to_all x1, starting transfers between devices, per_device(): lax.all_to_all(jnp.stack([vir_coeffs for _ in range(lax.axis_size('aux'))...  17.2 us
    dot_general x2, matrix products, per_device(): jnp.dot(amplitudes, flat_remote, preferred_element_type=jnp.float32)  13.3 us
    all_to_all x1, starting transfers between devices, per_device(): lax.all_to_all(by_virtual, 'aux', split_axis=1, concat_axis=2, tiled=True)  10.4 us
  transfers between devices with their start and end apart: 3, of which 3 were waited for; matrix products, arithmetic and copies ran while one was open for 1% of the time, Pallas kernels for 0%

profile of v1, /device:TPU:15, one launch (start us, length us, event | category | flops | bytes accessed | tf_op | source)
XLA Modules:
  0.0 512.6 jit_solution(7878513636239327724)
XLA Ops:
  6.5 3.0 stack.2
  9.5 17.2 %all-to-all-start = ((bf16[32,1408,40]{1,2,0:T(8,128)(2,1)}), bf16[32,1408,40]{1,2,0:T(8,128)(2,1)}, u32[]{:S(2)}, u32[]{:S(2)}) async-start(bf16[32,1408,40]{1,2,0:T(8,128)(2,1)} %stack.2), calls=%async_computation | async-start | bytes 7208960 | tf_op jit(solution)/shard_map/all_to_all | solution.py:21
  26.7 0.0 copy-done.2
  26.7 2.5 copy.15
  29.2 157.1 %all-to-all-done = bf16[32,1408,40]{1,2,0:T(8,128)(2,1)} async-done(((bf16[32,1408,40]{1,2,0:T(8,128)(2,1)}), bf16[32,1408,40]{1,2,0:T(8,128)(2,1)}, u32[]{:S(2)}, u32[]{:S(2)}) %all-to-all-start) | async-done | bytes 3604512 | tf_op jit(solution)/shard_map/all_to_all | solution.py:21
  186.3 7.2 %convolution_convert_fusion = bf16[1280,768]{0,1:T(8,128)(2,1)} fusion(bf16[1408,1280]{0,1:T(8,128)(2,1)} %bitcast.1, bf16[1408,768]{0,1:T(8,128)(2,1)} %bitcast.61), kind=kOutput, calls=%fused_computation.2 | convolution fusion | flops 2769223680 | bytes 7733248 | tf_op jit(solution)/shard_map/dot_general | solution.py:29
  193.5 3.9 copy.16
  197.4 35.3 %all_to_all.38 = bf16[1280,6,128]{2,1,0:T(8,128)(2,1)S(1)} all-to-all(bf16[1280,6,128]{2,1,0:T(8,128)(2,1)S(1)} %copy.16), channel_id=1, replica_groups=mesh['aux'=32,'pair'=16] {'pair'}, dimensions={0} | all-to-all | bytes 3932160 | tf_op jit(solution)/shard_map/all_to_all | solution.py:31
  232.7 1.5 copy.18
  234.2 10.4 %all-to-all-start.2 = ((bf16[80,96,128]{2,0,1:T(8,128)(2,1)}), bf16[80,96,128]{2,0,1:T(8,128)(2,1)S(1)}, u32[]{:S(2)}, u32[]{:S(2)}) async-start(bf16[80,96,128]{2,0,1:T(8,128)(2,1)} %bitcast.58), calls=%async_computation.2 | async-start | bytes 3932160 | tf_op jit(solution)/shard_map/all_to_all | solution.py:42
  244.6 0.2 all-reduce.3.cloned.1.call-start
  244.8 0.1 constant_dynamic-slice_fusion
  244.9 0.6 fusion.41
  246.7 89.0 %all-to-all-done.2 = bf16[80,96,128]{2,0,1:T(8,128)(2,1)S(1)} async-done(((bf16[80,96,128]{2,0,1:T(8,128)(2,1)}), bf16[80,96,128]{2,0,1:T(8,128)(2,1)S(1)}, u32[]{:S(2)}, u32[]{:S(2)}) %all-to-all-start.2) | async-done | bytes 1966112 | tf_op jit(solution)/shard_map/all_to_all | solution.py:42
  335.8 0.3 broadcast_select_fusion
  336.0 1.0 copy-done.1
  337.0 0.5 copy.21
  337.5 0.5 copy.20
  338.0 5.2 %copy_bitcast_fusion = (bf16[240,4096]{1,0:T(8,128)(2,1)}, bf16[240,4096]{1,0:T(8,128)(2,1)}) fusion(bf16[30,8,32,128]{3,2,1,0:T(8,128)(2,1)S(1)} %bitcast.59, bf16[30,8,32,128]{3,2,1,0:T(8,128)(2,1)S(1)} %bitcast.60), kind=kLoop, calls=%fused_computation.3 | loop fusion | bytes 7864320 | tf_op jit(solution)/shard_map/reshape | solution.py:51
  343.3 0.0 all-reduce.3.cloned.1.call-update
  344.6 0.1 dynamic_slice.26
  344.6 0.9 fusion.40
  345.5 0.1 broadcast_subtract_fusion
  345.6 0.2 sub.65
  345.8 0.2 sub.59
  345.9 0.2 sub.62
  346.1 2.1 copy.19
  348.1 137.9 %all-reduce.3.cloned.1.call-done = (bf16[240,4096]{1,0:T(8,128)(2,1)}, bf16[240,4096]{1,0:T(8,128)(2,1)}) async-done(((bf16[240,4096]{1,0:T(8,128)(2,1)}, bf16[240,4096]{1,0:T(8,128)(2,1)}), (bf16[240,4096]{1,0:T(8,128)(2,1)}, bf16[240,4096]{1,0:T(8,128)(2,1)})) %all-reduce.3.cloned.1.call-update) | async-done | bytes 3932176 | tf_op jit(solution)/shard_map/psum | solution.py:11
  486.0 6.4 %fusion.26 = f32[240,4096]{1,0:T(8,128)} fusion(bf16[240,4096]{1,0:T(8,128)(2,1)} %get-tuple-element.5, bf16[30,8,32,128]{3,2,1,0:T(8,128)(2,1)S(1)} %bitcast.53, f32[240]{0:T(256)S(1)} %sub.62, f32[240]{0:T(256)S(1)} %sub.59), kind=kOutput, calls=%fused_computation.19 | convolution fusion | flops 943948800 | bytes 7866240 | tf_op jit(solution)/shard_map/dot_general | solution.py:62
  492.4 7.0 %fusion = bf16[240,4096]{1,0:T(8,128)(2,1)} fusion(f32[240,4096]{1,0:T(8,128)} %fusion.26, bf16[240,4096]{1,0:T(8,128)(2,1)} %get-tuple-element.6, bf16[30,8,32,128]{3,2,1,0:T(8,128)(2,1)S(1)} %bitcast.54, f32[240]{0:T(256)S(1)} %sub.65, f32[240]{0:T(256)S(1)} %sub.59), kind=kOutput, calls=%fused_computation.1 | convolution fusion | flops 945914880 | bytes 9832320 | tf_op jit(solution)/shard_map/dot_general | solution.py:62
  499.4 3.7 reshape.90
  503.1 2.7 copy.22
  (6 shorter events, 0.0 us)
Async XLA Ops:
  6.5 238.3 %copy-start = (s32[32,2]{0,1:T(2,128)S(1)}, s32[32,2]{0,1:T(2,128)}, u32[]{:S(2)}) copy-start(s32[32,2]{0,1:T(2,128)} %param.9) | copy-start | bytes 772
  9.5 17.2 %copy-start.2 = (bf16[6,1408,128]{2,1,0:T(8,128)(2,1)S(1)}, bf16[6,1408,128]{2,1,0:T(8,128)(2,1)}, u32[]{:S(2)}) copy-start(bf16[6,1408,128]{2,1,0:T(8,128)(2,1)} %param.5) | copy-start | bytes 6488068
  9.5 176.8 %all-to-all-start = ((bf16[32,1408,40]{1,2,0:T(8,128)(2,1)}), bf16[32,1408,40]{1,2,0:T(8,128)(2,1)}, u32[]{:S(2)}, u32[]{:S(2)}) async-start(bf16[32,1408,40]{1,2,0:T(8,128)(2,1)} %stack.2), calls=%async_computation | async-start | bytes 7208960 | tf_op jit(solution)/shard_map/all_to_all | solution.py:21
  234.2 101.6 %all-to-all-start.2 = ((bf16[80,96,128]{2,0,1:T(8,128)(2,1)}), bf16[80,96,128]{2,0,1:T(8,128)(2,1)S(1)}, u32[]{:S(2)}, u32[]{:S(2)}) async-start(bf16[80,96,128]{2,0,1:T(8,128)(2,1)} %bitcast.58), calls=%async_computation.2 | async-start | bytes 3932160 | tf_op jit(solution)/shard_map/all_to_all | solution.py:42
  244.6 241.4 %all-reduce.3.cloned.1.call-start = ((), (), s32[]{:S(2)}) async-start(), calls=%async_computation.3 | async-start | bytes 7864320 | tf_op jit(solution)/shard_map/psum | solution.py:11
  335.8 1.3 copy-start.1
  343.3 1.3 copy-start.3
Sparse Core Ops, SparseCore 0:
  343.4 142.5 all-reduce.2
